TPU v7x, 32 devices: a whole 2x2x4 slice. The times are simulated.
32 devices in a mesh: pipe: 4 (over y, x), tensor: 8 (over z, core).
Axes of the slice: x: 2, y: 2, z: 4, core: 2. Of those that a mesh axis runs over, the one named last changes fastest.
Arguments:
- cotangent: bfloat16 [2, 128, 8192], P(None, 'tensor'), may hold values from -5 to 5
- inputs: bfloat16 [4, 2, 128, 8192], P('pipe', None, 'tensor'), may hold values from -24 to 24
- norm_gain: float32 [4, 8192], P('pipe'), may hold values from 0.1 to 1.9
- queries: bfloat16 [4, 2, 128, 4096], P('pipe', None, None, 'tensor'), may hold values from -4.6 to 4.6
- keys: bfloat16 [4, 2, 128, 4096], P('pipe', None, None, 'tensor'), may hold values from -4.6 to 4.6
- values: bfloat16 [4, 2, 128, 4096], P('pipe', None, None, 'tensor'), may hold values from -4 to 4
- qkv_weight: bfloat16 [4, 3, 8192, 4096], P('pipe', None, None, 'tensor'), may hold values from -0.0625 to 0.0625
- out_weight: bfloat16 [4, 4096, 8192], P('pipe', 'tensor'), may hold values from -0.09375 to 0.09375
- layout: int32 [2, 4, 4], replicated, may hold values from -1 to 3, as said below
Outputs:
- input_grads: bfloat16 [4, 2, 128, 8192], P('pipe', None, 'tensor')
Inputs may be any that keep to these rules, and one draw needn't show every extreme that they name: `layout`: each entry is -1 (no block) or a key block not after its query block; the last entry of query block i is i and the one before it is i - 1 (or -1 for block 0); the first two entries are two blocks of the micro-batch that all later query blocks attend to.
All inputs are finite; a program needn't handle non-finite values.
Results may differ from a plain program's by a relative error of at most 0.02.
Values may be sent and summed in bfloat16 or wider, within the bound.
A program may use at most 128 MiB of HBM per device.

v0:
```python
import math

import jax
import jax.numpy as jnp
from jax import lax
from jax.sharding import PartitionSpec as P

HD = 128


def shifted(value, axis, steps):
    count = lax.axis_size(axis)
    leading, last = (max(0, -steps), min(count, count - steps))
    return lax.ppermute(value, axis, [(source, source + steps) for source in range(leading, last)])


def token_mask(layout_rows, length):
    number = layout_rows.shape[0]
    num_blocks = layout_rows.shape[1]
    block_len = length // num_blocks
    blocks = jnp.arange(num_blocks, dtype=jnp.int32)
    listed = jnp.any(layout_rows[:, :, :, None] == blocks[None, None, None, :], axis=2)
    spread = jnp.broadcast_to(
        listed[:, :, None, :, None], (number, num_blocks, block_len, num_blocks, block_len)
    ).reshape(number, length, length)
    places = jnp.arange(length)
    return spread & (places[:, None] >= places[None, :])[None]


def local_grad(full_grad, first, queries, keys, values, out_weight, qkv_weight, layout):
    number = full_grad.shape[0]
    length = full_grad.shape[1]
    columns = queries.shape[2]
    heads_local = columns // HD
    scale = 1.0 / math.sqrt(HD)
    shape = (number, length, heads_local, HD)
    query = lax.dynamic_slice_in_dim(queries, first, number, 0).reshape(shape)
    key_rows = lax.dynamic_slice_in_dim(keys, first, number, 0).reshape(shape)
    value_rows = lax.dynamic_slice_in_dim(values, first, number, 0).reshape(shape)
    layout_rows = lax.dynamic_slice_in_dim(layout, first, number, 0)
    out_grad = lax.dot_general(
        full_grad, out_weight, (((2,), (1,)), ((), ())), preferred_element_type=jnp.float32
    ).astype(jnp.bfloat16)
    grad_heads = out_grad.reshape(shape)
    scores = (
        jnp.einsum("bqhd,bkhd->bhqk", query, key_rows, preferred_element_type=jnp.float32) * scale
    )
    allowed = token_mask(layout_rows, length)[:, None]
    scores = jnp.where(allowed, scores, -1e30)
    top = jnp.max(scores, axis=3, keepdims=True)
    expo = jnp.exp(scores - top)
    probs = expo / jnp.sum(expo, axis=3, keepdims=True)
    probs_half = probs.astype(jnp.bfloat16)
    attended = jnp.einsum(
        "bhqk,bkhd->bhqd", probs_half, value_rows, preferred_element_type=jnp.float32
    )
    delta = jnp.sum(attended * jnp.transpose(grad_heads, (0, 2, 1, 3)).astype(jnp.float32), axis=3)
    dprob = jnp.einsum(
        "bqhd,bkhd->bhqk", grad_heads, value_rows, preferred_element_type=jnp.float32
    )
    dscore = (probs * (dprob - delta[..., None])).astype(jnp.bfloat16)
    grad_query = (
        jnp.einsum("bhqk,bkhd->bqhd", dscore, key_rows, preferred_element_type=jnp.float32) * scale
    ).astype(jnp.bfloat16)
    grad_key = (
        jnp.einsum("bhqk,bqhd->bkhd", dscore, query, preferred_element_type=jnp.float32) * scale
    ).astype(jnp.bfloat16)
    grad_value = jnp.einsum(
        "bhqk,bqhd->bkhd", probs_half, grad_heads, preferred_element_type=jnp.float32
    ).astype(jnp.bfloat16)
    stacked = jnp.stack([grad_query, grad_key, grad_value], 1).reshape(number, 3, length, columns)
    return jnp.einsum("bcsn,cdn->bsd", stacked, qkv_weight, preferred_element_type=jnp.float32)


def norm_back(head_sum, x_rows, gain, grad_rows):
    x_float = x_rows.astype(jnp.float32)
    factor = lax.rsqrt(jnp.mean(x_float * x_float, axis=2, keepdims=True) + 1e-05)
    normed = x_float * factor
    scaled = head_sum * gain[None, None, :]
    through = factor * (scaled - normed * jnp.mean(scaled * normed, axis=2, keepdims=True))
    return (grad_rows.astype(jnp.float32) + through).astype(jnp.bfloat16)


def shards(cotangent, inputs, norm_gain, queries, keys, values, qkv_weight, out_weight, layout):
    sections = lax.axis_size("pipe")
    section = lax.axis_index("pipe")
    micro_total = cotangent.shape[0]
    rows_local = cotangent.shape[1]
    features = cotangent.shape[2]
    width = 1
    ticks = sections + micro_total - 1

    def placing(tick):
        first = tick - (sections - 1 - section)
        valid = (first >= 0) & (first < micro_total)
        return (jnp.clip(first, 0, micro_total - width), valid)

    def working(grad_rows, x_rows, first):
        full_grad = lax.all_gather(grad_rows, "tensor", axis=1, tiled=True)
        partial_value = local_grad(
            full_grad, first, queries[0], keys[0], values[0], out_weight[0], qkv_weight[0], layout
        )
        head_sum = lax.psum_scatter(
            partial_value.astype(jnp.bfloat16), "tensor", scatter_dimension=1, tiled=True
        ).astype(jnp.float32)
        return norm_back(head_sum, x_rows, norm_gain[0], grad_rows)

    def one_tick(tick, carry):
        outgoing, results = carry
        first, valid = placing(tick)
        incoming = shifted(outgoing, "pipe", -1)
        arriving = lax.dynamic_slice_in_dim(cotangent, first, width, 0)
        grad_rows = jnp.where(section == sections - 1, arriving, incoming)
        x_rows = lax.dynamic_slice_in_dim(inputs[0], first, width, 0)
        computed = working(grad_rows, x_rows, first)
        new_grad = jnp.where(valid, computed, grad_rows)
        previous = lax.dynamic_slice_in_dim(results, first, width, 0)
        results = lax.dynamic_update_slice_in_dim(
            results, jnp.where(valid, new_grad, previous), first, 0
        )
        return (new_grad, results)

    start_grad = jnp.zeros((width, rows_local, features), jnp.bfloat16)
    start_results = jnp.zeros((micro_total, rows_local, features), jnp.bfloat16)
    final_grad, results = lax.fori_loop(0, ticks, one_tick, (start_grad, start_results))
    return results[None]


def solution(mesh):
    in_specs = (
        P(None, "tensor", None),
        P("pipe", None, "tensor", None),
        P("pipe", None),
        P("pipe", None, None, "tensor"),
        P("pipe", None, None, "tensor"),
        P("pipe", None, None, "tensor"),
        P("pipe", None, None, "tensor"),
        P("pipe", "tensor", None),
        P(),
    )
    out_specs = P("pipe", None, "tensor", None)
    return jax.shard_map(shards, mesh=mesh, in_specs=in_specs, out_specs=out_specs, check_vma=False)
```

profile of v0, /device:TPU:0, one launch (start us, length us, event | category | flops | bytes accessed | tf_op | source)
XLA Modules:
  0.0 520.0 jit_solution(1277279147073431755)
XLA Ops:
  6.6 505.8 %while.18 = (s32[]{:T(128)}, bf16[1,16,8192]{2,1,0:T(8,128)(2,1)S(1)}, bf16[2,16,8192]{2,1,0:T(8,128)(2,1)S(1)}, s32[]{:T(128)}, pred[]{:T(512)}, /*index=5*/bf1...) while((s32[]{:T(128)}, ...), condition=%wide.region_8.9_spmd.clone, body=%wide.region_0.8_spmd.clone.sunk | while | flops 4401562624 | bytes 67811464 | solution.py:125
  6.7 1.3 collective-permute-start
  8.0 9.8 %collective-permute-done = bf16[1,16,8192]{2,1,0:T(8,128)(2,1)S(1)} collective-permute-done((bf16[1,16,8192]{2,1,0:T(8,128)(2,1)S(1)}, bf16[1,16,8192]{2,1,0:T(8,128)(2,1)S(1)}, u32[]{:S(2)}, u32[]{:S(2)}) %collective-permute-start) | collective-permute-done | bytes 262176 | tf_op jit(solution)/shard_map/while/body/eval_jaxpr/ppermute | solution.py:14
  17.8 1.7 dynamic-slice_select_fusion.2
  19.6 1.0 constant_dynamic-slice_fusion.5
  20.7 0.9 constant_dynamic-slice_fusion.6
  21.7 0.7 dynamic-slice_bitcast_fusion.2
  23.3 0.2 fusion.117
  23.5 26.7 %all-gather.2.cloned.1.call-done = bf16[1,128,8192]{2,1,0:T(8,128)(2,1)} async-done(((bf16[1,16,8192]{2,1,0:T(8,128)(2,1)}), bf16[1,128,8192]{2,1,0:T(8,128)(2,1)}) %all-gather.2.cloned.1.call-update) | async-done | bytes 2097168 | tf_op jit(solution)/shard_map/while/body/eval_jaxpr/all_gather | solution.py:99
  50.2 6.9 %fusion.113 = bf16[128,512]{1,0:T(8,128)(2,1)S(1)} fusion(bf16[1,512,8192]{2,1,0:T(8,128)(2,1)} %get-tuple-element.555, bf16[1,128,8192]{2,1,0:T(8,128)(2,1)} %all-gather.2.cloned.1.call-done), kind=kOutput, calls=%fused_computation.23.clone.1 | convolution fusion | flops 1073807360 | bytes 10616832 | tf_op jit(solution)/shard_map/while/body/eval_jaxpr/dot_general | solution.py:41
  59.3 14.5 %fusion.122 = bf16[1,128,8192]{2,1,0:T(8,128)(2,1)} fusion(bf16[1,3,8192,512]{3,2,1,0:T(8,128)(2,1)} %get-tuple-element.557, bf16[1,1,128,512]{3,2,1,0:T(8,128)(2,1)S(1)} %copy.97, bf16[1,1,128,512]{3,2,1,0:T(8,128)(2,1)S(1)} %copy.101, bf16[1,1,128,512]{3,2,1,0:T(8,128)(2,1)S(1)} %copy.103), kind=kOutput, calls=%fused_computation.5.clone.1 | convolution fusion | flops 3222667264 | bytes 27656192 | tf_op jit(solution)/shard_map/while/body/eval_jaxpr/bcsn,cdn->bsd/dot_general | solution.py:72
  74.0 35.2 %reduce-scatter.2.cloned.1.call-done = bf16[1,16,8192]{2,1,0:T(8,128)(2,1)} async-done(((bf16[1,128,8192]{2,1,0:T(8,128)(2,1)}), bf16[1,16,8192]{2,1,0:T(8,128)(2,1)}) %reduce-scatter.2.cloned.1.call-update) | async-done | bytes 262160 | tf_op jit(solution)/shard_map/while/body/eval_jaxpr/reduce_scatter | solution.py:103
  109.2 1.2 fusion.124
  110.4 1.3 select_dynamic-update-slice_fusion.2
  111.8 1.3 collective-permute-start
  113.1 7.0 %collective-permute-done = bf16[1,16,8192]{2,1,0:T(8,128)(2,1)S(1)} collective-permute-done((bf16[1,16,8192]{2,1,0:T(8,128)(2,1)S(1)}, bf16[1,16,8192]{2,1,0:T(8,128)(2,1)S(1)}, u32[]{:S(2)}, u32[]{:S(2)}) %collective-permute-start) | collective-permute-done | bytes 262176 | tf_op jit(solution)/shard_map/while/body/eval_jaxpr/ppermute | solution.py:14
  120.1 1.7 dynamic-slice_select_fusion.2
  121.8 1.0 constant_dynamic-slice_fusion.5
  123.0 0.9 constant_dynamic-slice_fusion.6
  124.0 0.7 dynamic-slice_bitcast_fusion.2
  125.5 0.2 fusion.117
  125.8 24.6 %all-gather.2.cloned.1.call-done = bf16[1,128,8192]{2,1,0:T(8,128)(2,1)} async-done(((bf16[1,16,8192]{2,1,0:T(8,128)(2,1)}), bf16[1,128,8192]{2,1,0:T(8,128)(2,1)}) %all-gather.2.cloned.1.call-update) | async-done | bytes 2097168 | tf_op jit(solution)/shard_map/while/body/eval_jaxpr/all_gather | solution.py:99
  150.4 6.9 %fusion.113 = bf16[128,512]{1,0:T(8,128)(2,1)S(1)} fusion(bf16[1,512,8192]{2,1,0:T(8,128)(2,1)} %get-tuple-element.555, bf16[1,128,8192]{2,1,0:T(8,128)(2,1)} %all-gather.2.cloned.1.call-done), kind=kOutput, calls=%fused_computation.23.clone.1 | convolution fusion | flops 1073807360 | bytes 10616832 | tf_op jit(solution)/shard_map/while/body/eval_jaxpr/dot_general | solution.py:41
  159.4 14.5 %fusion.122 = bf16[1,128,8192]{2,1,0:T(8,128)(2,1)} fusion(bf16[1,3,8192,512]{3,2,1,0:T(8,128)(2,1)} %get-tuple-element.557, bf16[1,1,128,512]{3,2,1,0:T(8,128)(2,1)S(1)} %copy.97, bf16[1,1,128,512]{3,2,1,0:T(8,128)(2,1)S(1)} %copy.101, bf16[1,1,128,512]{3,2,1,0:T(8,128)(2,1)S(1)} %copy.103), kind=kOutput, calls=%fused_computation.5.clone.1 | convolution fusion | flops 3222667264 | bytes 27656192 | tf_op jit(solution)/shard_map/while/body/eval_jaxpr/bcsn,cdn->bsd/dot_general | solution.py:72
  174.2 35.2 %reduce-scatter.2.cloned.1.call-done = bf16[1,16,8192]{2,1,0:T(8,128)(2,1)} async-done(((bf16[1,128,8192]{2,1,0:T(8,128)(2,1)}), bf16[1,16,8192]{2,1,0:T(8,128)(2,1)}) %reduce-scatter.2.cloned.1.call-update) | async-done | bytes 262160 | tf_op jit(solution)/shard_map/while/body/eval_jaxpr/reduce_scatter | solution.py:103
  209.4 1.2 fusion.124
  210.6 1.3 select_dynamic-update-slice_fusion.2
  212.0 1.3 collective-permute-start
  213.3 7.0 %collective-permute-done = bf16[1,16,8192]{2,1,0:T(8,128)(2,1)S(1)} collective-permute-done((bf16[1,16,8192]{2,1,0:T(8,128)(2,1)S(1)}, bf16[1,16,8192]{2,1,0:T(8,128)(2,1)S(1)}, u32[]{:S(2)}, u32[]{:S(2)}) %collective-permute-start) | collective-permute-done | bytes 262176 | tf_op jit(solution)/shard_map/while/body/eval_jaxpr/ppermute | solution.py:14
  220.2 1.7 dynamic-slice_select_fusion.2
  222.0 1.0 constant_dynamic-slice_fusion.5
  223.1 0.9 constant_dynamic-slice_fusion.6
  224.2 0.7 dynamic-slice_bitcast_fusion.2
  226.0 24.6 %all-gather.2.cloned.1.call-done = bf16[1,128,8192]{2,1,0:T(8,128)(2,1)} async-done(((bf16[1,16,8192]{2,1,0:T(8,128)(2,1)}), bf16[1,128,8192]{2,1,0:T(8,128)(2,1)}) %all-gather.2.cloned.1.call-update) | async-done | bytes 2097168 | tf_op jit(solution)/shard_map/while/body/eval_jaxpr/all_gather | solution.py:99
  250.5 6.9 %fusion.113 = bf16[128,512]{1,0:T(8,128)(2,1)S(1)} fusion(bf16[1,512,8192]{2,1,0:T(8,128)(2,1)} %get-tuple-element.555, bf16[1,128,8192]{2,1,0:T(8,128)(2,1)} %all-gather.2.cloned.1.call-done), kind=kOutput, calls=%fused_computation.23.clone.1 | convolution fusion | flops 1073807360 | bytes 10616832 | tf_op jit(solution)/shard_map/while/body/eval_jaxpr/dot_general | solution.py:41
  259.6 14.5 %fusion.122 = bf16[1,128,8192]{2,1,0:T(8,128)(2,1)} fusion(bf16[1,3,8192,512]{3,2,1,0:T(8,128)(2,1)} %get-tuple-element.557, bf16[1,1,128,512]{3,2,1,0:T(8,128)(2,1)S(1)} %copy.97, bf16[1,1,128,512]{3,2,1,0:T(8,128)(2,1)S(1)} %copy.101, bf16[1,1,128,512]{3,2,1,0:T(8,128)(2,1)S(1)} %copy.103), kind=kOutput, calls=%fused_computation.5.clone.1 | convolution fusion | flops 3222667264 | bytes 27656192 | tf_op jit(solution)/shard_map/while/body/eval_jaxpr/bcsn,cdn->bsd/dot_general | solution.py:72
  274.3 35.2 %reduce-scatter.2.cloned.1.call-done = bf16[1,16,8192]{2,1,0:T(8,128)(2,1)} async-done(((bf16[1,128,8192]{2,1,0:T(8,128)(2,1)}), bf16[1,16,8192]{2,1,0:T(8,128)(2,1)}) %reduce-scatter.2.cloned.1.call-update) | async-done | bytes 262160 | tf_op jit(solution)/shard_map/while/body/eval_jaxpr/reduce_scatter | solution.py:103
  309.5 1.2 fusion.124
  310.8 1.3 select_dynamic-update-slice_fusion.2
  312.1 1.3 collective-permute-start
  313.4 7.0 %collective-permute-done = bf16[1,16,8192]{2,1,0:T(8,128)(2,1)S(1)} collective-permute-done((bf16[1,16,8192]{2,1,0:T(8,128)(2,1)S(1)}, bf16[1,16,8192]{2,1,0:T(8,128)(2,1)S(1)}, u32[]{:S(2)}, u32[]{:S(2)}) %collective-permute-start) | collective-permute-done | bytes 262176 | tf_op jit(solution)/shard_map/while/body/eval_jaxpr/ppermute | solution.py:14
  320.4 1.7 dynamic-slice_select_fusion.2
  322.2 1.0 constant_dynamic-slice_fusion.5
  323.3 0.9 constant_dynamic-slice_fusion.6
  324.3 0.7 dynamic-slice_bitcast_fusion.2
  326.1 24.6 %all-gather.2.cloned.1.call-done = bf16[1,128,8192]{2,1,0:T(8,128)(2,1)} async-done(((bf16[1,16,8192]{2,1,0:T(8,128)(2,1)}), bf16[1,128,8192]{2,1,0:T(8,128)(2,1)}) %all-gather.2.cloned.1.call-update) | async-done | bytes 2097168 | tf_op jit(solution)/shard_map/while/body/eval_jaxpr/all_gather | solution.py:99
  350.7 6.9 %fusion.113 = bf16[128,512]{1,0:T(8,128)(2,1)S(1)} fusion(bf16[1,512,8192]{2,1,0:T(8,128)(2,1)} %get-tuple-element.555, bf16[1,128,8192]{2,1,0:T(8,128)(2,1)} %all-gather.2.cloned.1.call-done), kind=kOutput, calls=%fused_computation.23.clone.1 | convolution fusion | flops 1073807360 | bytes 10616832 | tf_op jit(solution)/shard_map/while/body/eval_jaxpr/dot_general | solution.py:41
  359.8 14.5 %fusion.122 = bf16[1,128,8192]{2,1,0:T(8,128)(2,1)} fusion(bf16[1,3,8192,512]{3,2,1,0:T(8,128)(2,1)} %get-tuple-element.557, bf16[1,1,128,512]{3,2,1,0:T(8,128)(2,1)S(1)} %copy.97, bf16[1,1,128,512]{3,2,1,0:T(8,128)(2,1)S(1)} %copy.101, bf16[1,1,128,512]{3,2,1,0:T(8,128)(2,1)S(1)} %copy.103), kind=kOutput, calls=%fused_computation.5.clone.1 | convolution fusion | flops 3222667264 | bytes 27656192 | tf_op jit(solution)/shard_map/while/body/eval_jaxpr/bcsn,cdn->bsd/dot_general | solution.py:72
  374.5 35.2 %reduce-scatter.2.cloned.1.call-done = bf16[1,16,8192]{2,1,0:T(8,128)(2,1)} async-done(((bf16[1,128,8192]{2,1,0:T(8,128)(2,1)}), bf16[1,16,8192]{2,1,0:T(8,128)(2,1)}) %reduce-scatter.2.cloned.1.call-update) | async-done | bytes 262160 | tf_op jit(solution)/shard_map/while/body/eval_jaxpr/reduce_scatter | solution.py:103
  409.7 1.2 fusion.124
  410.9 1.3 select_dynamic-update-slice_fusion.2
  412.3 1.3 collective-permute-start
  413.6 7.0 %collective-permute-done = bf16[1,16,8192]{2,1,0:T(8,128)(2,1)S(1)} collective-permute-done((bf16[1,16,8192]{2,1,0:T(8,128)(2,1)S(1)}, bf16[1,16,8192]{2,1,0:T(8,128)(2,1)S(1)}, u32[]{:S(2)}, u32[]{:S(2)}) %collective-permute-start) | collective-permute-done | bytes 262176 | tf_op jit(solution)/shard_map/while/body/eval_jaxpr/ppermute | solution.py:14
  420.6 1.7 dynamic-slice_select_fusion.2
  422.3 1.0 constant_dynamic-slice_fusion.5
  423.4 0.9 constant_dynamic-slice_fusion.6
  424.5 0.7 dynamic-slice_bitcast_fusion.2
  426.3 24.6 %all-gather.2.cloned.1.call-done = bf16[1,128,8192]{2,1,0:T(8,128)(2,1)} async-done(((bf16[1,16,8192]{2,1,0:T(8,128)(2,1)}), bf16[1,128,8192]{2,1,0:T(8,128)(2,1)}) %all-gather.2.cloned.1.call-update) | async-done | bytes 2097168 | tf_op jit(solution)/shard_map/while/body/eval_jaxpr/all_gather | solution.py:99
  450.9 6.9 %fusion.113 = bf16[128,512]{1,0:T(8,128)(2,1)S(1)} fusion(bf16[1,512,8192]{2,1,0:T(8,128)(2,1)} %get-tuple-element.555, bf16[1,128,8192]{2,1,0:T(8,128)(2,1)} %all-gather.2.cloned.1.call-done), kind=kOutput, calls=%fused_computation.23.clone.1 | convolution fusion | flops 1073807360 | bytes 10616832 | tf_op jit(solution)/shard_map/while/body/eval_jaxpr/dot_general | solution.py:41
  459.9 14.5 %fusion.122 = bf16[1,128,8192]{2,1,0:T(8,128)(2,1)} fusion(bf16[1,3,8192,512]{3,2,1,0:T(8,128)(2,1)} %get-tuple-element.557, bf16[1,1,128,512]{3,2,1,0:T(8,128)(2,1)S(1)} %copy.97, bf16[1,1,128,512]{3,2,1,0:T(8,128)(2,1)S(1)} %copy.101, bf16[1,1,128,512]{3,2,1,0:T(8,128)(2,1)S(1)} %copy.103), kind=kOutput, calls=%fused_computation.5.clone.1 | convolution fusion | flops 3222667264 | bytes 27656192 | tf_op jit(solution)/shard_map/while/body/eval_jaxpr/bcsn,cdn->bsd/dot_general | solution.py:72
  474.7 35.2 %reduce-scatter.2.cloned.1.call-done = bf16[1,16,8192]{2,1,0:T(8,128)(2,1)} async-done(((bf16[1,128,8192]{2,1,0:T(8,128)(2,1)}), bf16[1,16,8192]{2,1,0:T(8,128)(2,1)}) %reduce-scatter.2.cloned.1.call-update) | async-done | bytes 262160 | tf_op jit(solution)/shard_map/while/body/eval_jaxpr/reduce_scatter | solution.py:103
  509.9 1.2 fusion.124
  511.1 1.3 select_dynamic-update-slice_fusion.2
  512.4 0.8 copy-done.2
  (181 shorter events, 17.9 us)
Async XLA Ops:
  6.6 43.6 %all-gather.2.cloned.1.call-start = ((), (), s32[]{:S(2)}) async-start(), calls=%async_computation.1 | async-start | bytes 2359296 | tf_op jit(solution)/shard_map/while/body/eval_jaxpr/all_gather | solution.py:99
  6.7 11.1 %collective-permute-start = (bf16[1,16,8192]{2,1,0:T(8,128)(2,1)S(1)}, bf16[1,16,8192]{2,1,0:T(8,128)(2,1)S(1)}, u32[]{:S(2)}, u32[]{:S(2)}) collective-permute-start(bf16[1,16,8192]{2,1,0:T(8,128)(2,1)S(1)} %broadcast_select_fusion.2), channel_id=1, source_target_pairs={{8,0},{16,8},{24,16},{9,1},{17,9},{25,17},{10,2},{18,10},{26,18},{... | collective-permute-start | bytes 786440 | tf_op jit(solution)/shard_map/while/body/eval_jaxpr/ppermute | solution.py:14
  19.5 89.7 %reduce-scatter.2.cloned.1.call-start = ((), (), s32[]{:S(2)}) async-start(), calls=%async_computation.2 | async-start | bytes 2359296 | tf_op jit(solution)/shard_map/while/body/eval_jaxpr/reduce_scatter | solution.py:103
  59.2 14.6 %copy-start.1 = (bf16[1,2,16,8192]{3,2,1,0:T(8,128)(2,1)S(1)}, bf16[1,2,16,8192]{3,2,1,0:T(8,128)(2,1)}, u32[]{:S(2)}) copy-start(bf16[1,2,16,8192]{3,2,1,0:T(8,128)(2,1)} %get-tuple-element.551) | copy-start | bytes 1572868 | tf_op jit(solution)/shard_map/while
  59.3 50.0 %copy-start.3 = (f32[1,8192]{1,0:T(1,128)S(1)}, f32[1,8192]{1,0:T(1,128)}, u32[]{:S(2)}) copy-start(f32[1,8192]{1,0:T(1,128)} %get-tuple-element.558) | copy-start | bytes 98308 | tf_op jit(solution)/shard_map/while
  59.3 51.2 %copy-start = (bf16[1,16,8192]{2,1,0:T(8,128)(2,1)S(1)}, bf16[1,16,8192]{2,1,0:T(8,128)(2,1)}, u32[]{:S(2)}) copy-start(bf16[1,16,8192]{2,1,0:T(8,128)(2,1)} %dynamic-slice_select_fusion.2) | copy-start | bytes 786436 | tf_op jit(solution)/shard_map/while
  111.7 38.7 %all-gather.2.cloned.1.call-start = ((), (), s32[]{:S(2)}) async-start(), calls=%async_computation.1 | async-start | bytes 2359296 | tf_op jit(solution)/shard_map/while/body/eval_jaxpr/all_gather | solution.py:99
  111.8 8.3 %collective-permute-start = (bf16[1,16,8192]{2,1,0:T(8,128)(2,1)S(1)}, bf16[1,16,8192]{2,1,0:T(8,128)(2,1)S(1)}, u32[]{:S(2)}, u32[]{:S(2)}) collective-permute-start(bf16[1,16,8192]{2,1,0:T(8,128)(2,1)S(1)} %broadcast_select_fusion.2), channel_id=1, source_target_pairs={{8,0},{16,8},{24,16},{9,1},{17,9},{25,17},{10,2},{18,10},{26,18},{... | collective-permute-start | bytes 786440 | tf_op jit(solution)/shard_map/while/body/eval_jaxpr/ppermute | solution.py:14
  121.8 87.6 %reduce-scatter.2.cloned.1.call-start = ((), (), s32[]{:S(2)}) async-start(), calls=%async_computation.2 | async-start | bytes 2359296 | tf_op jit(solution)/shard_map/while/body/eval_jaxpr/reduce_scatter | solution.py:103
  159.4 14.6 %copy-start.1 = (bf16[1,2,16,8192]{3,2,1,0:T(8,128)(2,1)S(1)}, bf16[1,2,16,8192]{3,2,1,0:T(8,128)(2,1)}, u32[]{:S(2)}) copy-start(bf16[1,2,16,8192]{3,2,1,0:T(8,128)(2,1)} %get-tuple-element.551) | copy-start | bytes 1572868 | tf_op jit(solution)/shard_map/while
  159.4 50.0 %copy-start.3 = (f32[1,8192]{1,0:T(1,128)S(1)}, f32[1,8192]{1,0:T(1,128)}, u32[]{:S(2)}) copy-start(f32[1,8192]{1,0:T(1,128)} %get-tuple-element.558) | copy-start | bytes 98308 | tf_op jit(solution)/shard_map/while
  159.4 51.2 %copy-start = (bf16[1,16,8192]{2,1,0:T(8,128)(2,1)S(1)}, bf16[1,16,8192]{2,1,0:T(8,128)(2,1)}, u32[]{:S(2)}) copy-start(bf16[1,16,8192]{2,1,0:T(8,128)(2,1)} %dynamic-slice_select_fusion.2) | copy-start | bytes 786436 | tf_op jit(solution)/shard_map/while
  211.9 38.7 %all-gather.2.cloned.1.call-start = ((), (), s32[]{:S(2)}) async-start(), calls=%async_computation.1 | async-start | bytes 2359296 | tf_op jit(solution)/shard_map/while/body/eval_jaxpr/all_gather | solution.py:99
  212.0 8.3 %collective-permute-start = (bf16[1,16,8192]{2,1,0:T(8,128)(2,1)S(1)}, bf16[1,16,8192]{2,1,0:T(8,128)(2,1)S(1)}, u32[]{:S(2)}, u32[]{:S(2)}) collective-permute-start(bf16[1,16,8192]{2,1,0:T(8,128)(2,1)S(1)} %broadcast_select_fusion.2), channel_id=1, source_target_pairs={{8,0},{16,8},{24,16},{9,1},{17,9},{25,17},{10,2},{18,10},{26,18},{... | collective-permute-start | bytes 786440 | tf_op jit(solution)/shard_map/while/body/eval_jaxpr/ppermute | solution.py:14
  221.9 87.6 %reduce-scatter.2.cloned.1.call-start = ((), (), s32[]{:S(2)}) async-start(), calls=%async_computation.2 | async-start | bytes 2359296 | tf_op jit(solution)/shard_map/while/body/eval_jaxpr/reduce_scatter | solution.py:103
  259.6 14.6 %copy-start.1 = (bf16[1,2,16,8192]{3,2,1,0:T(8,128)(2,1)S(1)}, bf16[1,2,16,8192]{3,2,1,0:T(8,128)(2,1)}, u32[]{:S(2)}) copy-start(bf16[1,2,16,8192]{3,2,1,0:T(8,128)(2,1)} %get-tuple-element.551) | copy-start | bytes 1572868 | tf_op jit(solution)/shard_map/while
  259.6 50.0 %copy-start.3 = (f32[1,8192]{1,0:T(1,128)S(1)}, f32[1,8192]{1,0:T(1,128)}, u32[]{:S(2)}) copy-start(f32[1,8192]{1,0:T(1,128)} %get-tuple-element.558) | copy-start | bytes 98308 | tf_op jit(solution)/shard_map/while
  259.6 51.2 %copy-start = (bf16[1,16,8192]{2,1,0:T(8,128)(2,1)S(1)}, bf16[1,16,8192]{2,1,0:T(8,128)(2,1)}, u32[]{:S(2)}) copy-start(bf16[1,16,8192]{2,1,0:T(8,128)(2,1)} %dynamic-slice_select_fusion.2) | copy-start | bytes 786436 | tf_op jit(solution)/shard_map/while
  312.0 38.7 %all-gather.2.cloned.1.call-start = ((), (), s32[]{:S(2)}) async-start(), calls=%async_computation.1 | async-start | bytes 2359296 | tf_op jit(solution)/shard_map/while/body/eval_jaxpr/all_gather | solution.py:99
  312.1 8.3 %collective-permute-start = (bf16[1,16,8192]{2,1,0:T(8,128)(2,1)S(1)}, bf16[1,16,8192]{2,1,0:T(8,128)(2,1)S(1)}, u32[]{:S(2)}, u32[]{:S(2)}) collective-permute-start(bf16[1,16,8192]{2,1,0:T(8,128)(2,1)S(1)} %broadcast_select_fusion.2), channel_id=1, source_target_pairs={{8,0},{16,8},{24,16},{9,1},{17,9},{25,17},{10,2},{18,10},{26,18},{... | collective-permute-start | bytes 786440 | tf_op jit(solution)/shard_map/while/body/eval_jaxpr/ppermute | solution.py:14
  322.1 87.6 %reduce-scatter.2.cloned.1.call-start = ((), (), s32[]{:S(2)}) async-start(), calls=%async_computation.2 | async-start | bytes 2359296 | tf_op jit(solution)/shard_map/while/body/eval_jaxpr/reduce_scatter | solution.py:103
  359.7 14.6 %copy-start.1 = (bf16[1,2,16,8192]{3,2,1,0:T(8,128)(2,1)S(1)}, bf16[1,2,16,8192]{3,2,1,0:T(8,128)(2,1)}, u32[]{:S(2)}) copy-start(bf16[1,2,16,8192]{3,2,1,0:T(8,128)(2,1)} %get-tuple-element.551) | copy-start | bytes 1572868 | tf_op jit(solution)/shard_map/while
  359.7 50.0 %copy-start.3 = (f32[1,8192]{1,0:T(1,128)S(1)}, f32[1,8192]{1,0:T(1,128)}, u32[]{:S(2)}) copy-start(f32[1,8192]{1,0:T(1,128)} %get-tuple-element.558) | copy-start | bytes 98308 | tf_op jit(solution)/shard_map/while
  359.7 51.2 %copy-start = (bf16[1,16,8192]{2,1,0:T(8,128)(2,1)S(1)}, bf16[1,16,8192]{2,1,0:T(8,128)(2,1)}, u32[]{:S(2)}) copy-start(bf16[1,16,8192]{2,1,0:T(8,128)(2,1)} %dynamic-slice_select_fusion.2) | copy-start | bytes 786436 | tf_op jit(solution)/shard_map/while
  412.2 38.7 %all-gather.2.cloned.1.call-start = ((), (), s32[]{:S(2)}) async-start(), calls=%async_computation.1 | async-start | bytes 2359296 | tf_op jit(solution)/shard_map/while/body/eval_jaxpr/all_gather | solution.py:99
  412.3 8.3 %collective-permute-start = (bf16[1,16,8192]{2,1,0:T(8,128)(2,1)S(1)}, bf16[1,16,8192]{2,1,0:T(8,128)(2,1)S(1)}, u32[]{:S(2)}, u32[]{:S(2)}) collective-permute-start(bf16[1,16,8192]{2,1,0:T(8,128)(2,1)S(1)} %broadcast_select_fusion.2), channel_id=1, source_target_pairs={{8,0},{16,8},{24,16},{9,1},{17,9},{25,17},{10,2},{18,10},{26,18},{... | collective-permute-start | bytes 786440 | tf_op jit(solution)/shard_map/while/body/eval_jaxpr/ppermute | solution.py:14
  422.3 87.6 %reduce-scatter.2.cloned.1.call-start = ((), (), s32[]{:S(2)}) async-start(), calls=%async_computation.2 | async-start | bytes 2359296 | tf_op jit(solution)/shard_map/while/body/eval_jaxpr/reduce_scatter | solution.py:103
  459.9 14.6 %copy-start.1 = (bf16[1,2,16,8192]{3,2,1,0:T(8,128)(2,1)S(1)}, bf16[1,2,16,8192]{3,2,1,0:T(8,128)(2,1)}, u32[]{:S(2)}) copy-start(bf16[1,2,16,8192]{3,2,1,0:T(8,128)(2,1)} %get-tuple-element.551) | copy-start | bytes 1572868 | tf_op jit(solution)/shard_map/while
  459.9 50.0 %copy-start.3 = (f32[1,8192]{1,0:T(1,128)S(1)}, f32[1,8192]{1,0:T(1,128)}, u32[]{:S(2)}) copy-start(f32[1,8192]{1,0:T(1,128)} %get-tuple-element.558) | copy-start | bytes 98308 | tf_op jit(solution)/shard_map/while
  459.9 51.2 %copy-start = (bf16[1,16,8192]{2,1,0:T(8,128)(2,1)S(1)}, bf16[1,16,8192]{2,1,0:T(8,128)(2,1)}, u32[]{:S(2)}) copy-start(bf16[1,16,8192]{2,1,0:T(8,128)(2,1)} %dynamic-slice_select_fusion.2) | copy-start | bytes 786436 | tf_op jit(solution)/shard_map/while
  512.4 0.8 copy-start.2
Sparse Core Ops, SparseCore 0:
  19.6 30.5 all-gather.1
  73.9 35.2 reduce-scatter.1
  121.9 28.4 all-gather.1
  174.1 35.2 reduce-scatter.1
  222.1 28.4 all-gather.1
  274.2 35.2 reduce-scatter.1
  322.2 28.4 all-gather.1
  374.4 35.2 reduce-scatter.1
  422.4 28.4 all-gather.1
  474.5 35.2 reduce-scatter.1
where the time goes:
time: 521 us; the launch traced here: 520 us
  waiting for transfers between devices  339 us (65%)
  matrix products  114 us (22%)
  other arithmetic  23.8 us (5%)
  local copies, waits for them, and re-layouts  21.7 us (4%)
  between operations  13.4 us (3%)
  starting transfers between devices  6.87 us (1%)
    reduce_scatter x5, waiting for transfers between devices, working(): lax.psum_scatter(partial_value.astype(jnp.bfloat16), 'tensor', scatter_di...  176 us
    all_gather x5, waiting for transfers between devices, working(): full_grad = lax.all_gather(grad_rows, 'tensor', axis=1, tiled=True)  125 us
    dot_general x5, matrix products, local_grad(): jnp.einsum('bcsn,cdn->bsd', stacked, qkv_weight, preferred_element_type=j...  72.4 us
    ppermute x5, waiting for transfers between devices, shifted(): lax.ppermute(value, axis, [(source, source + steps) for source in range(l...  37.7 us
    dot_general x5, matrix products, local_grad(): lax.dot_general(full_grad, out_weight, (((2,), (1,)), ((), ())), preferre...  34.7 us
  transfers between devices with their start and end apart: 15, of which 15 were waited for; matrix products, arithmetic and copies ran while one was open for 4% of the time, Pallas kernels for 0%

commit v1 on v0

v1 whole, which is shorter than its diff:
```python
import functools
import math

import jax
import jax.numpy as jnp
from jax import lax
from jax.experimental import pallas as pl
from jax.experimental.pallas import tpu as pltpu
from jax.sharding import PartitionSpec as P

HD = 128
MESH = pl.DeviceIdType.MESH
NT = (((1,), (1,)), ((), ()))
TN = (((0,), (0,)), ((), ()))
NN = (((1,), (0,)), ((), ()))


def mm(a, b, dims):
    return lax.dot_general(a, b, dims, preferred_element_type=jnp.float32)


def body(
    sizes,
    layout, cot, xs, gain, qs, ks, vs, wqkv_hbm, wout_hbm,
    out,
    wqkv, wout, full, part, sibs, zsum, zgot, acc, grads, head,
    wout_sem, wqkv_sem, ag_s, ag_r, sg_s, sg_r, rb_s, rb_r, rz_s, rz_r, hop_s, hop_r,
):
    S, T, M, R, D, C, L, K, J, SUB = sizes
    Z = T // 2
    ck = D // K
    cj = D // J
    s = lax.axis_index("pipe")
    t = lax.axis_index("tensor")
    z = t // 2
    c = t % 2
    sib = z * 2 + (1 - c)
    scale = 1.0 / math.sqrt(HD)

    def kcols(k):
        return pl.ds(pl.multiple_of(k * ck, ck), ck)

    def jcols(j):
        return pl.ds(pl.multiple_of(j * cj, cj), cj)

    def peer(dz):
        return lax.rem(z + dz, Z) * 2 + c

    def origin(dz):
        return lax.rem(z + (Z - dz), Z) * 2 + c

    def wout_copy(k):
        return pltpu.make_async_copy(
            wout_hbm.at[0, :, kcols(k)], wout.at[:, kcols(k)], wout_sem.at[k]
        )

    def wqkv_copy(j):
        return pltpu.make_async_copy(
            wqkv_hbm.at[0, :, jcols(j), :], wqkv.at[:, jcols(j), :], wqkv_sem.at[j]
        )

    def remote(src, dst, ss, rs, device):
        return pltpu.make_async_remote_copy(
            src_ref=src, dst_ref=dst, send_sem=ss, recv_sem=rs,
            device_id=device, device_id_type=MESH,
        )

    def ag_out(m, k, dz):
        ref = full.at[m, t, :, kcols(k)]
        return remote(ref, ref, ag_s.at[m, k, dz - 1], ag_r.at[m, k, dz - 1], (s, peer(dz)))

    def ag_in(m, k, dz):
        ref = full.at[m, origin(dz), :, kcols(k)]
        return remote(ref, ref, ag_s.at[m, k, dz - 1], ag_r.at[m, k, dz - 1], (s, peer(dz)))

    def sg_out(m, k, dz):
        ref = full.at[m, origin(dz), :, kcols(k)]
        return remote(ref, ref, sg_s.at[m, k, dz], sg_r.at[m, k, dz], (s, sib))

    def sg_in(m, k, dz):
        ref = full.at[m, origin(dz) + 1 - 2 * c, :, kcols(k)]
        return remote(ref, ref, sg_s.at[m, k, dz], sg_r.at[m, k, dz], (s, sib))

    def rb(m, j):
        return remote(
            part.at[m, 1 - c, :, :, jcols(j)], sibs.at[m, :, :, jcols(j)],
            rb_s.at[m, j], rb_r.at[m, j], (s, sib),
        )

    def rz(m, j, dz):
        return remote(
            zsum.at[m, lax.rem(z + dz, Z), :, jcols(j)], zgot.at[m, dz - 1, :, jcols(j)],
            rz_s.at[m, j, dz - 1], rz_r.at[m, j, dz - 1], (s, peer(dz)),
        )

    def hop(m, k, section):
        return remote(
            out.at[m, :, kcols(k)], full.at[m, t, :, kcols(k)],
            hop_s.at[m, k], hop_r.at[m, k], (section, t),
        )

    def loop(n, fn):
        def step(i, carry):
            fn(i)
            return carry
        lax.fori_loop(0, n, step, 0)

    barrier = pltpu.get_barrier_semaphore()
    for dz in range(1, Z):
        pl.semaphore_signal(barrier, inc=1, device_id=(s, peer(dz)), device_id_type=MESH)
    pl.semaphore_signal(barrier, inc=1, device_id=(s, sib), device_id_type=MESH)

    @pl.when(s > 0)
    def _():
        pl.semaphore_signal(barrier, inc=1, device_id=(s - 1, t), device_id_type=MESH)

    @pl.when(s < S - 1)
    def _():
        pl.semaphore_signal(barrier, inc=1, device_id=(s + 1, t), device_id_type=MESH)

    loop(K, lambda k: wout_copy(k).start())
    loop(J, lambda j: wqkv_copy(j).start())
    ends = jnp.where(s == 0, 1, 0) + jnp.where(s == S - 1, 1, 0)
    pl.semaphore_wait(barrier, Z + 2 - ends)

    def micro(m):
        @pl.when(s == S - 1)
        def _():
            full[m, t] = cot[m]

        def spread(k):
            @pl.when(s < S - 1)
            def _():
                hop(m, k, s + 1).wait_recv()

            for dz in range(1, Z):
                ag_out(m, k, dz).start()
            sg_out(m, k, 0).start()

        loop(K, spread)
        acc[...] = jnp.zeros_like(acc)

        def gather(k):
            for dz in range(1, Z):
                ag_in(m, k, dz).wait_recv()
                sg_out(m, k, dz).start()

            @pl.when(m == 0)
            def _():
                wout_copy(k).wait()

            for dz in range(Z):
                sg_in(m, k, dz).wait_recv()
            rows = full[m, :, :, kcols(k)].reshape(L, ck)
            acc[...] += mm(rows, wout[:, kcols(k)], NT)

        loop(K, gather)

        nb = layout.shape[1]
        bl = L // nb
        kb = lax.broadcasted_iota(jnp.int32, (bl, L), 1) // bl
        strips = []
        for b in range(nb):
            strip = kb == layout[m, b, 0]
            for e in range(1, layout.shape[2]):
                strip = strip | (kb == layout[m, b, e])
            strips.append(jnp.where(strip, 1.0, 0.0))
        listed = jnp.concatenate(strips, axis=0)
        row = lax.broadcasted_iota(jnp.int32, (L, L), 0)
        col = lax.broadcasted_iota(jnp.int32, (L, L), 1)
        allowed = (listed > 0.5) & (col <= row)

        for h in range(C // HD):
            hc = slice(h * HD, (h + 1) * HD)
            query = qs[m, :, hc]
            key = ks[m, :, hc]
            value = vs[m, :, hc]
            go32 = acc[:, hc].astype(jnp.bfloat16)
            scores = jnp.where(allowed, mm(query, key, NT) * scale, -1e30)
            expo = jnp.exp(scores - jnp.max(scores, axis=1, keepdims=True))
            probs = expo / jnp.sum(expo, axis=1, keepdims=True)
            half = probs.astype(jnp.bfloat16)
            attended = mm(half, value, NN)
            delta = jnp.sum(attended * go32.astype(jnp.float32), axis=1, keepdims=True)
            dprob = mm(go32, value, NT)
            dscore = (probs * (dprob - delta)).astype(jnp.bfloat16)
            grads[0, :, hc] = (mm(dscore, key, NN) * scale).astype(jnp.bfloat16)
            grads[1, :, hc] = (mm(dscore, query, TN) * scale).astype(jnp.bfloat16)
            grads[2, :, hc] = mm(half, go32, TN).astype(jnp.bfloat16)

        def pair_sum(j):
            rb(m, j).wait_recv()

            def piece(i):
                cols = pl.ds(pl.multiple_of(j * cj + i * SUB, SUB), SUB)
                total = part[m, c, :, :, cols].astype(jnp.float32)
                total = total + sibs[m, :, :, cols].astype(jnp.float32)
                zsum[m, :, :, cols] = total.astype(jnp.bfloat16)

            loop(cj // SUB, piece)
            for dz in range(1, Z):
                rz(m, j, dz).start()

        def produce(j):
            @pl.when(m == 0)
            def _():
                wqkv_copy(j).wait()

            def piece(i):
                cols = pl.ds(pl.multiple_of(j * cj + i * SUB, SUB), SUB)
                value = mm(grads[0], wqkv[0, cols, :], NT)
                value = value + mm(grads[1], wqkv[1, cols, :], NT)
                value = value + mm(grads[2], wqkv[2, cols, :], NT)
                value = value.astype(jnp.bfloat16)
                for o in range(T):
                    part[m, o % 2, o // 2, :, cols] = value[o * R : (o + 1) * R]

            loop(cj // SUB, piece)
            rb(m, j).start()

            @pl.when(j > 0)
            def _():
                pair_sum(j - 1)

        loop(J, produce)
        pair_sum(J - 1)

        def settle(j, carry):
            for dz in range(1, Z):
                rz(m, j, dz).wait_recv()

            def piece(i, carry):
                squares, dots = carry
                cols = pl.ds(pl.multiple_of(j * cj + i * SUB, SUB), SUB)
                total = zsum[m, z, :, cols].astype(jnp.float32)
                for dz in range(1, Z):
                    total = total + zgot[m, dz - 1, :, cols].astype(jnp.float32)
                scaled = total * gain[:, cols]
                head[:, cols] = scaled
                x = xs[0, m, :, cols].astype(jnp.float32)
                squares = squares + jnp.sum(x * x, axis=1, keepdims=True)
                dots = dots + jnp.sum(x * scaled, axis=1, keepdims=True)
                return squares, dots

            return lax.fori_loop(0, cj // SUB, piece, carry)

        zero = jnp.zeros((R, 1), jnp.float32)
        squares, dots = lax.fori_loop(0, J, settle, (zero, zero))
        factor = lax.rsqrt(squares / D + 1e-05)
        inner = factor * factor * (dots / D)

        def finish(k):
            def piece(i):
                cols = pl.ds(pl.multiple_of(k * ck + i * SUB, SUB), SUB)
                x = xs[0, m, :, cols].astype(jnp.float32)
                through = factor * (head[:, cols] - x * inner)
                out[m, :, cols] = (
                    full[m, t, :, cols].astype(jnp.float32) + through
                ).astype(jnp.bfloat16)

            loop(ck // SUB, piece)

            @pl.when(s > 0)
            def _():
                hop(m, k, s - 1).start()

        loop(K, finish)

    loop(M, micro)

    def drain(m):
        def drain_k(k):
            for dz in range(1, Z):
                ag_out(m, k, dz).wait_send()
            for dz in range(Z):
                sg_out(m, k, dz).wait_send()

            @pl.when(s > 0)
            def _():
                hop(m, k, s - 1).wait_send()

        def drain_j(j):
            rb(m, j).wait_send()
            for dz in range(1, Z):
                rz(m, j, dz).wait_send()

        loop(K, drain_k)
        loop(J, drain_j)

    loop(M, drain)


def solution(mesh):
    S = mesh.shape["pipe"]
    T = mesh.shape["tensor"]

    def shards(cotangent, inputs, norm_gain, queries, keys, values, qkv_weight, out_weight, layout):
        M, R, D = cotangent.shape
        C = queries.shape[3]
        L = queries.shape[2]
        Z = T // 2
        K = 4
        J = 4
        SUB = 512
        sizes = (S, T, M, R, D, C, L, K, J, SUB)
        vmem = pl.BlockSpec(memory_space=pltpu.VMEM)
        hbm = pl.BlockSpec(memory_space=pl.ANY)
        bf = jnp.bfloat16
        dma = pltpu.SemaphoreType.DMA
        result = pl.pallas_call(
            functools.partial(body, sizes),
            out_shape=jax.ShapeDtypeStruct((M, R, D), bf),
            in_specs=[pl.BlockSpec(memory_space=pltpu.SMEM)] + [vmem] * 6 + [hbm] * 2,
            out_specs=vmem,
            scratch_shapes=[
                pltpu.VMEM((3, D, C), bf),
                pltpu.VMEM((C, D), bf),
                pltpu.VMEM((M, T, R, D), bf),
                pltpu.VMEM((M, 2, Z, R, D), bf),
                pltpu.VMEM((M, Z, R, D), bf),
                pltpu.VMEM((M, Z, R, D), bf),
                pltpu.VMEM((M, Z - 1, R, D), bf),
                pltpu.VMEM((L, C), jnp.float32),
                pltpu.VMEM((3, L, C), bf),
                pltpu.VMEM((R, D), jnp.float32),
                dma((K,)),
                dma((J,)),
                dma((M, K, Z - 1)),
                dma((M, K, Z - 1)),
                dma((M, K, Z)),
                dma((M, K, Z)),
                dma((M, J)),
                dma((M, J)),
                dma((M, J, Z - 1)),
                dma((M, J, Z - 1)),
                dma((M, K)),
                dma((M, K)),
            ],
            compiler_params=pltpu.CompilerParams(
                collective_id=0, has_side_effects=True, vmem_limit_bytes=60 * 1024 * 1024
            ),
        )(
            layout, cotangent, inputs, norm_gain, queries[0], keys[0], values[0],
            qkv_weight, out_weight,
        )
        return result[None]

    in_specs = (
        P(None, "tensor", None),
        P("pipe", None, "tensor", None),
        P("pipe", None),
        P("pipe", None, None, "tensor"),
        P("pipe", None, None, "tensor"),
        P("pipe", None, None, "tensor"),
        P("pipe", None, None, "tensor"),
        P("pipe", "tensor", None),
        P(),
    )
    out_specs = P("pipe", None, "tensor", None)
    return jax.shard_map(shards, mesh=mesh, in_specs=in_specs, out_specs=out_specs, check_vma=False)
```

time: 521 us -> 311 us (0.60)
  waiting for transfers between devices: 339 us -> 0 us
  Pallas kernels: 0 us -> 309 us
  matrix products: 114 us -> 0 us
  other arithmetic: 23.8 us -> 0 us
  local copies, waits for them, and re-layouts: 21.7 us -> 1.87 us
  between operations: 13.4 us -> 0.01 us
  starting transfers between devices: 6.87 us -> 0 us
    pallas_call x0 -> x1, Pallas kernels: none -> 309 us  [shards(): pl.pallas_call(functools.partial(body, sizes), out_shape=jax.ShapeDtypeSt...]
    reduce_scatter x5 -> x0, waiting for transfers between devices: 176 us -> none  [working(): lax.psum_scatter(partial_value.astype(jnp.bfloat16), 'tensor', scatter_di...]
    all_gather x5 -> x0, waiting for transfers between devices: 125 us -> none  [working(): full_grad = lax.all_gather(grad_rows, 'tensor', axis=1, tiled=True)]
    dot_general x40 -> x0, matrix products: 114 us -> none  [the longest x5 72.4 us: local_grad(): jnp.einsum('bcsn,cdn->bsd', stacked, qkv_weight, preferred_element_type=j...]
    ppermute x5 -> x0, waiting for transfers between devices: 37.7 us -> none  [shifted(): lax.ppermute(value, axis, [(source, source + steps) for source in range(l...]
    dynamic_slice x25 -> x0, local copies, waits for them, and re-layouts: 11.4 us -> none  [the longest x10 5.58 us: local_grad(): lax.dynamic_slice_in_dim(values, first, number, 0).reshape(shape)]
    select_n x5 -> x0, other arithmetic: 8.41 us -> none  [one_tick(): grad_rows = jnp.where(section == sections - 1, arriving, incoming)]
    reduce_sum x10 -> x0, other arithmetic: 7.03 us -> none  [the longest x5 6.05 us: norm_back(): jnp.mean(scaled * normed, axis=2, keepdims=True)]
  transfers between devices with their start and end apart: 15 -> 0, of which waited for: 15 -> 0; matrix products, arithmetic and copies ran while one was open for 4% -> 0% of each run, Pallas kernels for 0% -> 0%
where the time goes in v1:
time: 311 us
  Pallas kernels  309 us (99%)
    pallas_call x1, Pallas kernels, shards(): pl.pallas_call(functools.partial(body, sizes), out_shape=jax.ShapeDtypeSt...  309 us

profile of v1, /device:TPU:0, one launch (start us, length us, event | category | flops | bytes accessed | tf_op | source)
XLA Modules:
  0.0 310.5 jit_solution(12393218928941590128)
XLA Ops:
  0.0 308.7 %shard_map.91 = bf16[2,16,8192]{2,1,0:T(8,128)(2,1)} custom-call(s32[2,4,4]{2,1,0:T(4,128)} %layout.1, bf16[2,16,8192]{2,1,0:T(8,128)(2,1)} %cot.1, bf16[1,2,16,8192]{3,2,1,0:T(8,128)(2,1)} %xs.1, f32[1,8192]{1,0:T(1,128)} %gain.1, bf16[2,128,512]{2,1,0:T(8,128)(2,1)} %bitcast.5, bf16[2,128,512]{2,1,0:T(8,128)(2,1)} %bitcast.6, ...), custom_call_target="tpu_custom_call" | custom-call | tf_op jit(solution)/shard_map/pallas_call | solution.py:310
  308.7 1.9 copy.11

commit v2 on v1

--- a/solution.py
+++ b/solution.py
@@ -23,10 +23,11 @@
     sizes,
     layout, cot, xs, gain, qs, ks, vs, wqkv_hbm, wout_hbm,
     out,
-    wqkv, wout, full, part, sibs, zsum, zgot, acc, grads, head,
+    wqkv, wout, full, part, sibs, zsum, zgot, acc, grads, head, passed, probs_keep, att_keep,
     wout_sem, wqkv_sem, ag_s, ag_r, sg_s, sg_r, rb_s, rb_r, rz_s, rz_r, hop_s, hop_r,
+    ra_s, ra_r, rf_s, rf_r,
 ):
-    S, T, M, R, D, C, L, K, J, SUB = sizes
+    S, T, M, R, D, C, L, K, KB, J, SUB = sizes
     Z = T // 2
     ck = D // K
     cj = D // J
@@ -99,6 +100,21 @@
             hop_s.at[m, k], hop_r.at[m, k], (section, t),
         )
 
+    def acols(k):
+        return pl.ds(pl.multiple_of((k - KB) * ck, ck), ck)
+
+    def ra(m, k, dz):
+        return remote(
+            out.at[m, :, kcols(k)], passed.at[m, dz - 1, :, acols(k)],
+            ra_s.at[m, k - KB, dz - 1], ra_r.at[m, k - KB, dz - 1], (s, peer(dz)),
+        )
+
+    def rf(m, k, dz, section):
+        return remote(
+            passed.at[m, dz - 1, :, acols(k)], full.at[m, origin(dz), :, kcols(k)],
+            rf_s.at[m, k - KB, dz - 1], rf_r.at[m, k - KB, dz - 1], (section, t),
+        )
+
     def loop(n, fn):
         def step(i, carry):
             fn(i)
@@ -123,7 +139,7 @@
     ends = jnp.where(s == 0, 1, 0) + jnp.where(s == S - 1, 1, 0)
     pl.semaphore_wait(barrier, Z + 2 - ends)
 
-    def micro(m):
+    def begin(m):
         @pl.when(s == S - 1)
         def _():
             full[m, t] = cot[m]
@@ -133,29 +149,21 @@
             def _():
                 hop(m, k, s + 1).wait_recv()
 
-            for dz in range(1, Z):
-                ag_out(m, k, dz).start()
+            @pl.when((s == S - 1) | (k < KB))
+            def _():
+                for dz in range(1, Z):
+                    ag_out(m, k, dz).start()
+
             sg_out(m, k, 0).start()
 
         loop(K, spread)
+
+    def micro(m):
+        @pl.when((s < S - 1) | (m == 0))
+        def _():
+            begin(m)
+
         acc[...] = jnp.zeros_like(acc)
-
-        def gather(k):
-            for dz in range(1, Z):
-                ag_in(m, k, dz).wait_recv()
-                sg_out(m, k, dz).start()
-
-            @pl.when(m == 0)
-            def _():
-                wout_copy(k).wait()
-
-            for dz in range(Z):
-                sg_in(m, k, dz).wait_recv()
-            rows = full[m, :, :, kcols(k)].reshape(L, ck)
-            acc[...] += mm(rows, wout[:, kcols(k)], NT)
-
-        loop(K, gather)
-
         nb = layout.shape[1]
         bl = L // nb
         kb = lax.broadcasted_iota(jnp.int32, (bl, L), 1) // bl
@@ -172,16 +180,45 @@
 
         for h in range(C // HD):
             hc = slice(h * HD, (h + 1) * HD)
+            scores = jnp.where(allowed, mm(qs[m, :, hc], ks[m, :, hc], NT) * scale, -1e30)
+            expo = jnp.exp(scores - jnp.max(scores, axis=1, keepdims=True))
+            probs = expo / jnp.sum(expo, axis=1, keepdims=True)
+            probs_keep[h] = probs
+            att_keep[:, hc] = mm(probs.astype(jnp.bfloat16), vs[m, :, hc], NN)
+
+        def gather(k):
+            for dz in range(1, Z):
+
+                @pl.when((s == S - 1) | (k < KB))
+                def _():
+                    ag_in(m, k, dz).wait_recv()
+
+                @pl.when((s < S - 1) & (k >= KB))
+                def _():
+                    rf(m, k, dz, s + 1).wait_recv()
+
+                sg_out(m, k, dz).start()
+
+            @pl.when(m == 0)
+            def _():
+                wout_copy(k).wait()
+
+            for dz in range(Z):
+                sg_in(m, k, dz).wait_recv()
+            rows = full[m, :, :, kcols(k)].reshape(L, ck)
+            acc[...] += mm(rows, wout[:, kcols(k)], NT)
+
+        loop(K, gather)
+
+        for h in range(C // HD):
+            hc = slice(h * HD, (h + 1) * HD)
             query = qs[m, :, hc]
             key = ks[m, :, hc]
             value = vs[m, :, hc]
             go32 = acc[:, hc].astype(jnp.bfloat16)
-            scores = jnp.where(allowed, mm(query, key, NT) * scale, -1e30)
-            expo = jnp.exp(scores - jnp.max(scores, axis=1, keepdims=True))
-            probs = expo / jnp.sum(expo, axis=1, keepdims=True)
+            probs = probs_keep[h]
             half = probs.astype(jnp.bfloat16)
-            attended = mm(half, value, NN)
-            delta = jnp.sum(attended * go32.astype(jnp.float32), axis=1, keepdims=True)
+            delta = jnp.sum(att_keep[:, hc] * go32.astype(jnp.float32), axis=1, keepdims=True)
             dprob = mm(go32, value, NT)
             dscore = (probs * (dprob - delta)).astype(jnp.bfloat16)
             grads[0, :, hc] = (mm(dscore, key, NN) * scale).astype(jnp.bfloat16)
@@ -224,6 +261,10 @@
 
         loop(J, produce)
         pair_sum(J - 1)
+
+        @pl.when((s == S - 1) & (m < M - 1))
+        def _():
+            begin(m + 1)
 
         def settle(j, carry):
             for dz in range(1, Z):
@@ -264,20 +305,43 @@
             def _():
                 hop(m, k, s - 1).start()
 
+                @pl.when(k >= KB)
+                def _():
+                    for dz in range(1, Z):
+                        ra(m, k, dz).start()
+
         loop(K, finish)
+
+        def pass_on(i):
+            for dz in range(1, Z):
+                ra(m, KB + i, dz).wait_recv()
+                rf(m, KB + i, dz, s - 1).start()
+
+        @pl.when(s > 0)
+        def _():
+            loop(K - KB, pass_on)
 
     loop(M, micro)
 
     def drain(m):
         def drain_k(k):
-            for dz in range(1, Z):
-                ag_out(m, k, dz).wait_send()
+            @pl.when((s == S - 1) | (k < KB))
+            def _():
+                for dz in range(1, Z):
+                    ag_out(m, k, dz).wait_send()
+
             for dz in range(Z):
                 sg_out(m, k, dz).wait_send()
 
             @pl.when(s > 0)
             def _():
                 hop(m, k, s - 1).wait_send()
+
+                @pl.when(k >= KB)
+                def _():
+                    for dz in range(1, Z):
+                        ra(m, k, dz).wait_send()
+                        rf(m, k, dz, s - 1).wait_send()
 
         def drain_j(j):
             rb(m, j).wait_send()
@@ -300,9 +364,10 @@
         L = queries.shape[2]
         Z = T // 2
         K = 4
-        J = 4
+        KB = 2
+        J = 8
         SUB = 512
-        sizes = (S, T, M, R, D, C, L, K, J, SUB)
+        sizes = (S, T, M, R, D, C, L, K, KB, J, SUB)
         vmem = pl.BlockSpec(memory_space=pltpu.VMEM)
         hbm = pl.BlockSpec(memory_space=pl.ANY)
         bf = jnp.bfloat16
@@ -323,6 +388,9 @@
                 pltpu.VMEM((L, C), jnp.float32),
                 pltpu.VMEM((3, L, C), bf),
                 pltpu.VMEM((R, D), jnp.float32),
+                pltpu.VMEM((M, Z - 1, R, (K - KB) * (D // K)), bf),
+                pltpu.VMEM((C // HD, L, L), jnp.float32),
+                pltpu.VMEM((L, C), jnp.float32),
                 dma((K,)),
                 dma((J,)),
                 dma((M, K, Z - 1)),
@@ -335,6 +403,10 @@
                 dma((M, J, Z - 1)),
                 dma((M, K)),
                 dma((M, K)),
+                dma((M, K - KB, Z - 1)),
+                dma((M, K - KB, Z - 1)),
+                dma((M, K - KB, Z - 1)),
+                dma((M, K - KB, Z - 1)),
             ],
             compiler_params=pltpu.CompilerParams(
                 collective_id=0, has_side_effects=True, vmem_limit_bytes=60 * 1024 * 1024

time: 311 us -> 294 us (0.945)
  Pallas kernels: 309 us -> 292 us
    pallas_call x1, Pallas kernels: 309 us -> 292 us  [shards(): pl.pallas_call(functools.partial(body, sizes), out_shape=jax.ShapeDtypeSt...]
where the time goes in v2:
time: 294 us
  Pallas kernels  292 us (99%)
    pallas_call x1, Pallas kernels, shards(): pl.pallas_call(functools.partial(body, sizes), out_shape=jax.ShapeDtypeSt...  292 us

profile of v2, /device:TPU:0, one launch (start us, length us, event | category | flops | bytes accessed | tf_op | source)
XLA Modules:
  0.0 293.7 jit_solution(14334063993502404182)
XLA Ops:
  0.0 291.9 %shard_map.91 = bf16[2,16,8192]{2,1,0:T(8,128)(2,1)} custom-call(s32[2,4,4]{2,1,0:T(4,128)} %layout.1, bf16[2,16,8192]{2,1,0:T(8,128)(2,1)} %cot.1, bf16[1,2,16,8192]{3,2,1,0:T(8,128)(2,1)} %xs.1, f32[1,8192]{1,0:T(1,128)} %gain.1, bf16[2,128,512]{2,1,0:T(8,128)(2,1)} %bitcast.5, bf16[2,128,512]{2,1,0:T(8,128)(2,1)} %bitcast.6, ...), custom_call_target="tpu_custom_call" | custom-call | tf_op jit(solution)/shard_map/pallas_call | solution.py:375
  291.9 1.9 copy.11

commit v3 on v2

--- a/solution.py
+++ b/solution.py
@@ -23,9 +23,9 @@
     sizes,
     layout, cot, xs, gain, qs, ks, vs, wqkv_hbm, wout_hbm,
     out,
-    wqkv, wout, full, part, sibs, zsum, zgot, acc, grads, head, passed, probs_keep, att_keep,
+    wqkv, wout, full, part, sibs, zsum, zgot, acc, grads, head, passed, cpassed, probs_keep, att_keep,
     wout_sem, wqkv_sem, ag_s, ag_r, sg_s, sg_r, rb_s, rb_r, rz_s, rz_r, hop_s, hop_r,
-    ra_s, ra_r, rf_s, rf_r,
+    ra_s, ra_r, rf_s, rf_r, ca_s, ca_r, cf_s,
 ):
     S, T, M, R, D, C, L, K, KB, J, SUB = sizes
     Z = T // 2
@@ -100,19 +100,34 @@
             hop_s.at[m, k], hop_r.at[m, k], (section, t),
         )
 
-    def acols(k):
-        return pl.ds(pl.multiple_of((k - KB) * ck, ck), ck)
+    def early(m, k):
+        return (k >= KB) | (m == M - 1)
+
+    def late(m, k):
+        return (k < KB) & (m < M - 1)
 
     def ra(m, k, dz):
         return remote(
-            out.at[m, :, kcols(k)], passed.at[m, dz - 1, :, acols(k)],
-            ra_s.at[m, k - KB, dz - 1], ra_r.at[m, k - KB, dz - 1], (s, peer(dz)),
+            out.at[m, :, kcols(k)], passed.at[m, dz - 1, :, kcols(k)],
+            ra_s.at[m, k, dz - 1], ra_r.at[m, k, dz - 1], (s, peer(dz)),
         )
 
     def rf(m, k, dz, section):
         return remote(
-            passed.at[m, dz - 1, :, acols(k)], full.at[m, origin(dz), :, kcols(k)],
-            rf_s.at[m, k - KB, dz - 1], rf_r.at[m, k - KB, dz - 1], (section, t),
+            passed.at[m, dz - 1, :, kcols(k)], full.at[m, origin(dz), :, kcols(k)],
+            rf_s.at[m, k, dz - 1], rf_r.at[m, k, dz - 1], (section, t),
+        )
+
+    def ca(m, k, dz):
+        return remote(
+            cot.at[m, :, kcols(k)], cpassed.at[m, dz - 1, :, kcols(k)],
+            ca_s.at[m, k, dz - 1], ca_r.at[m, k, dz - 1], (s, peer(dz)),
+        )
+
+    def cf(m, k, dz):
+        return remote(
+            cpassed.at[m, dz - 1, :, kcols(k)], full.at[m, origin(dz), :, kcols(k)],
+            cf_s.at[m, k, dz - 1], rf_r.at[m, k, dz - 1], (s + 1, t),
         )
 
     def loop(n, fn):
@@ -139,6 +154,29 @@
     ends = jnp.where(s == 0, 1, 0) + jnp.where(s == S - 1, 1, 0)
     pl.semaphore_wait(barrier, Z + 2 - ends)
 
+    source = jnp.where(s == S - 1, s - 1, s + 1)
+
+    def each(fn):
+        def outer(m):
+            def inner(k):
+                @pl.when(early(m, k))
+                def _():
+                    for dz in range(1, Z):
+                        fn(m, k, dz)
+
+            loop(K, inner)
+
+        loop(M, outer)
+
+    def relay(m, k, dz):
+        ca(m, k, dz).wait_recv()
+        cf(m, k, dz).start()
+
+    @pl.when(s == S - 2)
+    def _():
+        each(lambda m, k, dz: ca(m, k, dz).start())
+        each(relay)
+
     def begin(m):
         @pl.when(s == S - 1)
         def _():
@@ -149,7 +187,7 @@
             def _():
                 hop(m, k, s + 1).wait_recv()
 
-            @pl.when((s == S - 1) | (k < KB))
+            @pl.when(late(m, k))
             def _():
                 for dz in range(1, Z):
                     ag_out(m, k, dz).start()
@@ -159,9 +197,7 @@
         loop(K, spread)
 
     def micro(m):
-        @pl.when((s < S - 1) | (m == 0))
-        def _():
-            begin(m)
+        begin(m)
 
         acc[...] = jnp.zeros_like(acc)
         nb = layout.shape[1]
@@ -189,13 +225,13 @@
         def gather(k):
             for dz in range(1, Z):
 
-                @pl.when((s == S - 1) | (k < KB))
+                @pl.when(late(m, k))
                 def _():
                     ag_in(m, k, dz).wait_recv()
 
-                @pl.when((s < S - 1) & (k >= KB))
+                @pl.when(early(m, k))
                 def _():
-                    rf(m, k, dz, s + 1).wait_recv()
+                    rf(m, k, dz, source).wait_recv()
 
                 sg_out(m, k, dz).start()
 
@@ -262,10 +298,6 @@
         loop(J, produce)
         pair_sum(J - 1)
 
-        @pl.when((s == S - 1) & (m < M - 1))
-        def _():
-            begin(m + 1)
-
         def settle(j, carry):
             for dz in range(1, Z):
                 rz(m, j, dz).wait_recv()
@@ -305,27 +337,29 @@
             def _():
                 hop(m, k, s - 1).start()
 
-                @pl.when(k >= KB)
+                @pl.when(early(m, k))
                 def _():
                     for dz in range(1, Z):
                         ra(m, k, dz).start()
 
         loop(K, finish)
 
-        def pass_on(i):
-            for dz in range(1, Z):
-                ra(m, KB + i, dz).wait_recv()
-                rf(m, KB + i, dz, s - 1).start()
+        def pass_on(k):
+            @pl.when(early(m, k))
+            def _():
+                for dz in range(1, Z):
+                    ra(m, k, dz).wait_recv()
+                    rf(m, k, dz, s - 1).start()
 
         @pl.when(s > 0)
         def _():
-            loop(K - KB, pass_on)
+            loop(K, pass_on)
 
     loop(M, micro)
 
     def drain(m):
         def drain_k(k):
-            @pl.when((s == S - 1) | (k < KB))
+            @pl.when(late(m, k))
             def _():
                 for dz in range(1, Z):
                     ag_out(m, k, dz).wait_send()
@@ -337,7 +371,7 @@
             def _():
                 hop(m, k, s - 1).wait_send()
 
-                @pl.when(k >= KB)
+                @pl.when(early(m, k))
                 def _():
                     for dz in range(1, Z):
                         ra(m, k, dz).wait_send()
@@ -352,6 +386,14 @@
         loop(J, drain_j)
 
     loop(M, drain)
+
+    def drain_relay(m, k, dz):
+        ca(m, k, dz).wait_send()
+        cf(m, k, dz).wait_send()
+
+    @pl.when(s == S - 2)
+    def _():
+        each(drain_relay)
 
 
 def solution(mesh):
@@ -388,7 +430,8 @@
                 pltpu.VMEM((L, C), jnp.float32),
                 pltpu.VMEM((3, L, C), bf),
                 pltpu.VMEM((R, D), jnp.float32),
-                pltpu.VMEM((M, Z - 1, R, (K - KB) * (D // K)), bf),
+                pltpu.VMEM((M, Z - 1, R, D), bf),
+                pltpu.VMEM((M, Z - 1, R, D), bf),
                 pltpu.VMEM((C // HD, L, L), jnp.float32),
                 pltpu.VMEM((L, C), jnp.float32),
                 dma((K,)),
@@ -403,10 +446,13 @@
                 dma((M, J, Z - 1)),
                 dma((M, K)),
                 dma((M, K)),
-                dma((M, K - KB, Z - 1)),
-                dma((M, K - KB, Z - 1)),
-                dma((M, K - KB, Z - 1)),
-                dma((M, K - KB, Z - 1)),
+                dma((M, K, Z - 1)),
+                dma((M, K, Z - 1)),
+                dma((M, K, Z - 1)),
+                dma((M, K, Z - 1)),
+                dma((M, K, Z - 1)),
+                dma((M, K, Z - 1)),
+                dma((M, K, Z - 1)),
             ],
             compiler_params=pltpu.CompilerParams(
                 collective_id=0, has_side_effects=True, vmem_limit_bytes=60 * 1024 * 1024

time: 294 us -> 296 us (level)
  no operation moved by 1% of the time
where the time goes in v3:
time: 296 us; the launch traced here: 295 us
  Pallas kernels  294 us (99%)
    pallas_call x1, Pallas kernels, shards(): pl.pallas_call(functools.partial(body, sizes), out_shape=jax.ShapeDtypeSt...  294 us

profile of v3, /device:TPU:0, one launch (start us, length us, event | category | flops | bytes accessed | tf_op | source)
XLA Modules:
  0.0 295.4 jit_solution(14725370270257957576)
XLA Ops:
  0.0 293.6 %shard_map.91 = bf16[2,16,8192]{2,1,0:T(8,128)(2,1)} custom-call(s32[2,4,4]{2,1,0:T(4,128)} %layout.1, bf16[2,16,8192]{2,1,0:T(8,128)(2,1)} %cot.1, bf16[1,2,16,8192]{3,2,1,0:T(8,128)(2,1)} %xs.1, f32[1,8192]{1,0:T(1,128)} %gain.1, bf16[2,128,512]{2,1,0:T(8,128)(2,1)} %bitcast.5, bf16[2,128,512]{2,1,0:T(8,128)(2,1)} %bitcast.6, ...), custom_call_target="tpu_custom_call" | custom-call | tf_op jit(solution)/shard_map/pallas_call | solution.py:417
  293.6 1.9 copy.11

commit v4 on v3

--- a/solution.py
+++ b/solution.py
@@ -101,10 +101,10 @@
         )
 
     def early(m, k):
-        return (k >= KB) | (m == M - 1)
+        return k >= KB
 
     def late(m, k):
-        return (k < KB) & (m < M - 1)
+        return k < KB
 
     def ra(m, k, dz):
         return remote(
@@ -405,8 +405,8 @@
         C = queries.shape[3]
         L = queries.shape[2]
         Z = T // 2
-        K = 4
-        KB = 2
+        K = 8
+        KB = 4
         J = 8
         SUB = 512
         sizes = (S, T, M, R, D, C, L, K, KB, J, SUB)

time: 296 us -> 286 us (0.966)
  Pallas kernels: 294 us -> 284 us
    pallas_call x1, Pallas kernels: 294 us -> 284 us  [shards(): pl.pallas_call(functools.partial(body, sizes), out_shape=jax.ShapeDtypeSt...]
where the time goes in v4:
time: 286 us
  Pallas kernels  284 us (99%)
    pallas_call x1, Pallas kernels, shards(): pl.pallas_call(functools.partial(body, sizes), out_shape=jax.ShapeDtypeSt...  284 us

profile of v4, /device:TPU:0, one launch (start us, length us, event | category | flops | bytes accessed | tf_op | source)
XLA Modules:
  0.0 285.6 jit_solution(13915049630957863218)
XLA Ops:
  0.0 283.7 %shard_map.91 = bf16[2,16,8192]{2,1,0:T(8,128)(2,1)} custom-call(s32[2,4,4]{2,1,0:T(4,128)} %layout.1, bf16[2,16,8192]{2,1,0:T(8,128)(2,1)} %cot.1, bf16[1,2,16,8192]{3,2,1,0:T(8,128)(2,1)} %xs.1, f32[1,8192]{1,0:T(1,128)} %gain.1, bf16[2,128,512]{2,1,0:T(8,128)(2,1)} %bitcast.5, bf16[2,128,512]{2,1,0:T(8,128)(2,1)} %bitcast.6, ...), custom_call_target="tpu_custom_call" | custom-call | tf_op jit(solution)/shard_map/pallas_call | solution.py:417
  283.7 1.9 copy.11
